TPU v7x, 128 devices: a whole 4x4x4 slice. The times are simulated.
128 devices in a mesh: ctx: 32 (over y, z, x_lo), seq: 2 (over core), fsdp: 2 (over x_hi).
Axes of the slice: x: 4 (x_hi: 2, x_lo: 2; x = x_hi * 2 + x_lo), y: 4, z: 4, core: 2. Of those that a mesh axis runs over, the one named last changes fastest.
Arguments:
- tokens: bfloat16 [4, 4096, 768], P(('seq', 'fsdp'), 'ctx'), may hold values from -6 to 6
- cotangent: bfloat16 [4, 4096, 768], P(('seq', 'fsdp'), 'ctx'), may hold values from -6 to 6
- w_query: bfloat16 [768, 768], P('fsdp'), may hold values from -0.21875 to 0.21875
- w_key: bfloat16 [768, 768], P('fsdp'), may hold values from -0.21875 to 0.21875
- w_value: bfloat16 [768, 768], P('fsdp'), may hold values from -0.21875 to 0.21875
- w_output: bfloat16 [768, 768], P('fsdp'), may hold values from -6 to 6
- b_query: bfloat16 [768], P('fsdp'), may hold values from -1.5 to 1.5
- b_value: bfloat16 [768], P('fsdp'), may hold values from -0.15625 to 0.15625
- b_output: bfloat16 [768], P('fsdp'), may hold values from -1.5 to 1.5
- first_gain: bfloat16 [768], P('fsdp'), may hold values from 0.5 to 1.5
- first_shift: bfloat16 [768], P('fsdp'), may hold values from -1.5 to 1.5
- w_inner: bfloat16 [768, 3072], P('fsdp'), may hold values from -0.21875 to 0.21875
- b_inner: bfloat16 [3072], P('fsdp'), may hold values from -1.5 to 1.5
- w_outer: bfloat16 [3072, 768], P('fsdp'), may hold values from -0.109375 to 0.109375
- b_outer: bfloat16 [768], P('fsdp'), may hold values from -1.5 to 1.5
- second_gain: bfloat16 [768], P('fsdp'), may hold values from 0.5 to 1.5
- second_shift: bfloat16 [768], P('fsdp'), may hold values from -1.5 to 1.5
Outputs:
- layer_out: bfloat16 [4, 4096, 768], P(('seq', 'fsdp'), 'ctx')
- tokens_grad: float32 [4, 4096, 768], P(('seq', 'fsdp'), 'ctx')
- w_query_grad: float32 [768, 768], P('fsdp')
- w_key_grad: float32 [768, 768], P('fsdp')
- w_value_grad: float32 [768, 768], P('fsdp')
- w_output_grad: float32 [768, 768], P('fsdp')
- b_query_grad: float32 [768], P('fsdp')
- b_value_grad: float32 [768], P('fsdp')
- b_output_grad: float32 [768], P('fsdp')
- first_gain_grad: float32 [768], P('fsdp')
- first_shift_grad: float32 [768], P('fsdp')
- w_inner_grad: float32 [768, 3072], P('fsdp')
- b_inner_grad: float32 [3072], P('fsdp')
- w_outer_grad: float32 [3072, 768], P('fsdp')
- b_outer_grad: float32 [768], P('fsdp')
- second_gain_grad: float32 [768], P('fsdp')
- second_shift_grad: float32 [768], P('fsdp')
All inputs are finite; a program needn't handle non-finite values.
Results may differ from a plain program's by a relative error of at most 0.022.
Values may be sent and summed in bfloat16 or wider, within the bound.
A program may use at most 192 MiB of HBM per device.

v0:
```python
import functools
import jax
import jax.numpy as jnp
from jax import lax
from jax.sharding import PartitionSpec as P

HEADS = 12
HEAD_DIM = 64
epsilon = 1e-12


def product(left, right):
    return jnp.dot(left, right, preferred_element_type=jnp.float32)


def product_left(left, right):
    return lax.dot_general(
        left, right, (((0,), (0,)), ((), ())), preferred_element_type=jnp.float32
    )


def product_right(left, right):
    return lax.dot_general(
        left, right, (((1,), (1,)), ((), ())), preferred_element_type=jnp.float32
    )


def layer_norm(hidden, gain, shift):
    centred = hidden - jnp.mean(hidden, axis=-1, keepdims=True)
    inverse = lax.rsqrt(jnp.mean(centred * centred, axis=-1, keepdims=True) + epsilon)
    normal = centred * inverse
    return (normal * gain + shift, normal, inverse)


def norm_back(grad, normal, inverse, gain):
    scaled = grad * gain
    centre = jnp.mean(scaled, axis=-1, keepdims=True)
    along = jnp.mean(scaled * normal, axis=-1, keepdims=True)
    return inverse * (scaled - centre - normal * along)


def group_slice(array, index):
    columns = 2 * HEAD_DIM
    piece = lax.dynamic_slice_in_dim(array, index * columns, columns, 2)
    return piece.reshape(piece.shape[0], piece.shape[1], 2, HEAD_DIM)


def scores_of(query, keys):
    return jnp.einsum(
        "sqhd,skhd->shqk", query, keys, preferred_element_type=jnp.float32
    ) * HEAD_DIM ** (-0.5)


def flatten_group(array):
    return array.reshape(array.shape[0], array.shape[1], 2 * HEAD_DIM)


def to_rows(stacked):
    groups, seqs, count, columns = stacked.shape
    return stacked.transpose(1, 2, 0, 3).reshape(seqs * count, groups * columns)


def local(
    tokens,
    cotangent,
    w_query,
    w_key,
    w_value,
    w_output,
    b_query,
    b_value,
    b_output,
    first_gain,
    first_shift,
    w_inner,
    b_inner,
    w_outer,
    b_outer,
    second_gain,
    second_shift,
):
    seqs, block, width = tokens.shape
    rows = seqs * block
    indices = jnp.arange(HEADS // 2)
    scale = HEAD_DIM ** (-0.5)
    w_query, w_key, w_value, w_output, b_query, b_value, b_output, first_gain, first_shift = (
        lax.all_gather(w_query, "fsdp", axis=0, tiled=True),
        lax.all_gather(w_key, "fsdp", axis=0, tiled=True),
        lax.all_gather(w_value, "fsdp", axis=0, tiled=True),
        lax.all_gather(w_output, "fsdp", axis=0, tiled=True),
        lax.all_gather(b_query, "fsdp", axis=0, tiled=True),
        lax.all_gather(b_value, "fsdp", axis=0, tiled=True),
        lax.all_gather(b_output, "fsdp", axis=0, tiled=True),
        lax.all_gather(first_gain, "fsdp", axis=0, tiled=True),
        lax.all_gather(first_shift, "fsdp", axis=0, tiled=True),
    )
    flat = tokens.reshape(rows, width)
    query = (product(flat, w_query) + b_query).astype(jnp.bfloat16).reshape(seqs, block, width)
    keys = product(flat, w_key).astype(jnp.bfloat16).reshape(seqs, block, width)
    values = (product(flat, w_value) + b_value).astype(jnp.bfloat16).reshape(seqs, block, width)
    keys_all, values_all = (
        lax.all_gather(keys, "ctx", axis=1, tiled=True),
        lax.all_gather(values, "ctx", axis=1, tiled=True),
    )

    def forward_group(index):
        scores = scores_of(group_slice(query, index), group_slice(keys_all, index))
        top = jnp.max(scores, axis=-1, keepdims=True)
        weights = jnp.exp(scores - top)
        total = jnp.sum(weights, axis=-1, keepdims=True)
        probs = (weights / total).astype(jnp.bfloat16)
        mixed = jnp.einsum(
            "shqk,skhd->sqhd",
            probs,
            group_slice(values_all, index),
            preferred_element_type=jnp.float32,
        )
        return (flatten_group(mixed), (top + jnp.log(total))[..., 0])

    mixed, logsum = lax.map(forward_group, indices)
    attended = to_rows(mixed).astype(jnp.bfloat16)
    first_in = flat.astype(jnp.float32) + product(attended, w_output) + b_output
    normed, first_normal, first_inverse = layer_norm(first_in, first_gain, first_shift)
    normed_low = normed.astype(jnp.bfloat16)
    w_inner, b_inner, w_outer, b_outer, second_gain, second_shift = (
        lax.all_gather(w_inner, "fsdp", axis=0, tiled=True),
        lax.all_gather(b_inner, "fsdp", axis=0, tiled=True),
        lax.all_gather(w_outer, "fsdp", axis=0, tiled=True),
        lax.all_gather(b_outer, "fsdp", axis=0, tiled=True),
        lax.all_gather(second_gain, "fsdp", axis=0, tiled=True),
        lax.all_gather(second_shift, "fsdp", axis=0, tiled=True),
    )
    gelu_exact = functools.partial(jax.nn.gelu, approximate=False)
    inner = product(normed_low, w_inner) + b_inner
    active = gelu_exact(inner).astype(jnp.bfloat16)
    second_in = normed + product(active, w_outer) + b_outer
    layer_out, second_normal, second_inverse = layer_norm(second_in, second_gain, second_shift)
    grad_out = cotangent.reshape(rows, width).astype(jnp.float32)
    second_scale = jnp.sum(grad_out * second_normal, axis=0)
    second_offset = jnp.sum(grad_out, axis=0)
    grad_second = norm_back(grad_out, second_normal, second_inverse, second_gain)
    outer_low = grad_second.astype(jnp.bfloat16)
    outer_matrix = product_left(active, outer_low)
    outer_bias = jnp.sum(outer_low.astype(jnp.float32), axis=0)
    slope = jax.vjp(gelu_exact, inner)[1](product_right(outer_low, w_outer))[0]
    inner_low = slope.astype(jnp.bfloat16)
    inner_matrix = product_left(normed_low, inner_low)
    inner_bias = jnp.sum(inner_low.astype(jnp.float32), axis=0)
    grad_normed = grad_second + product_right(inner_low, w_inner)
    first_scale = jnp.sum(grad_normed * first_normal, axis=0)
    first_offset = jnp.sum(grad_normed, axis=0)
    grad_first = norm_back(grad_normed, first_normal, first_inverse, first_gain)
    branch_low = grad_first.astype(jnp.bfloat16)
    output_matrix = product_left(attended, branch_low)
    output_bias = jnp.sum(branch_low.astype(jnp.float32), axis=0)
    upstream = product_right(branch_low, w_output).astype(jnp.bfloat16).reshape(seqs, block, width)

    def backward_group(pair):
        index, group_logsum = pair
        query_part = group_slice(query, index)
        keys_part = group_slice(keys_all, index)
        values_part = group_slice(values_all, index)
        upstream_part = group_slice(upstream, index)
        probs = jnp.exp(scores_of(query_part, keys_part) - group_logsum[..., None])
        prob_grads = jnp.einsum(
            "sqhd,skhd->shqk", upstream_part, values_part, preferred_element_type=jnp.float32
        )
        row_dot = jnp.sum(probs * prob_grads, axis=-1, keepdims=True)
        score_low = (probs * (prob_grads - row_dot)).astype(jnp.bfloat16)
        query_grad = (
            jnp.einsum("shqk,skhd->sqhd", score_low, keys_part, preferred_element_type=jnp.float32)
            * scale
        )
        key_grad = (
            jnp.einsum("shqk,sqhd->skhd", score_low, query_part, preferred_element_type=jnp.float32)
            * scale
        )
        value_grad = jnp.einsum(
            "shqk,sqhd->skhd",
            probs.astype(jnp.bfloat16),
            upstream_part,
            preferred_element_type=jnp.float32,
        )
        return (flatten_group(query_grad), flatten_group(key_grad), flatten_group(value_grad))

    query_grads, key_terms, value_terms = lax.map(backward_group, (indices, logsum))
    key_grads, value_grads = (
        lax.psum_scatter(
            key_terms.astype(jnp.bfloat16), "ctx", scatter_dimension=2, tiled=True
        ).astype(jnp.float32),
        lax.psum_scatter(
            value_terms.astype(jnp.bfloat16), "ctx", scatter_dimension=2, tiled=True
        ).astype(jnp.float32),
    )
    query_low = to_rows(query_grads).astype(jnp.bfloat16)
    key_low = to_rows(key_grads).astype(jnp.bfloat16)
    value_low = to_rows(value_grads).astype(jnp.bfloat16)
    query_matrix = product_left(flat, query_low)
    query_bias = jnp.sum(query_low.astype(jnp.float32), axis=0)
    keys_matrix = product_left(flat, key_low)
    value_matrix = product_left(flat, value_low)
    value_bias = jnp.sum(value_low.astype(jnp.float32), axis=0)
    tokens_grad = (
        grad_first
        + product_right(query_low, w_query)
        + product_right(key_low, w_key)
        + product_right(value_low, w_value)
    )
    (
        query_matrix,
        keys_matrix,
        value_matrix,
        output_matrix,
        query_bias,
        value_bias,
        output_bias,
        first_scale,
        first_offset,
        inner_matrix,
        inner_bias,
        outer_matrix,
        outer_bias,
        second_scale,
        second_offset,
    ) = (
        lax.psum_scatter(
            query_matrix.astype(jnp.bfloat16), "fsdp", scatter_dimension=0, tiled=True
        ).astype(jnp.float32),
        lax.psum_scatter(
            keys_matrix.astype(jnp.bfloat16), "fsdp", scatter_dimension=0, tiled=True
        ).astype(jnp.float32),
        lax.psum_scatter(
            value_matrix.astype(jnp.bfloat16), "fsdp", scatter_dimension=0, tiled=True
        ).astype(jnp.float32),
        lax.psum_scatter(
            output_matrix.astype(jnp.bfloat16), "fsdp", scatter_dimension=0, tiled=True
        ).astype(jnp.float32),
        lax.psum_scatter(
            query_bias.astype(jnp.bfloat16), "fsdp", scatter_dimension=0, tiled=True
        ).astype(jnp.float32),
        lax.psum_scatter(
            value_bias.astype(jnp.bfloat16), "fsdp", scatter_dimension=0, tiled=True
        ).astype(jnp.float32),
        lax.psum_scatter(
            output_bias.astype(jnp.bfloat16), "fsdp", scatter_dimension=0, tiled=True
        ).astype(jnp.float32),
        lax.psum_scatter(
            first_scale.astype(jnp.bfloat16), "fsdp", scatter_dimension=0, tiled=True
        ).astype(jnp.float32),
        lax.psum_scatter(
            first_offset.astype(jnp.bfloat16), "fsdp", scatter_dimension=0, tiled=True
        ).astype(jnp.float32),
        lax.psum_scatter(
            inner_matrix.astype(jnp.bfloat16), "fsdp", scatter_dimension=0, tiled=True
        ).astype(jnp.float32),
        lax.psum_scatter(
            inner_bias.astype(jnp.bfloat16), "fsdp", scatter_dimension=0, tiled=True
        ).astype(jnp.float32),
        lax.psum_scatter(
            outer_matrix.astype(jnp.bfloat16), "fsdp", scatter_dimension=0, tiled=True
        ).astype(jnp.float32),
        lax.psum_scatter(
            outer_bias.astype(jnp.bfloat16), "fsdp", scatter_dimension=0, tiled=True
        ).astype(jnp.float32),
        lax.psum_scatter(
            second_scale.astype(jnp.bfloat16), "fsdp", scatter_dimension=0, tiled=True
        ).astype(jnp.float32),
        lax.psum_scatter(
            second_offset.astype(jnp.bfloat16), "fsdp", scatter_dimension=0, tiled=True
        ).astype(jnp.float32),
    )
    finals = lax.psum(
        (
            query_matrix,
            keys_matrix,
            value_matrix,
            output_matrix,
            query_bias,
            value_bias,
            output_bias,
            first_scale,
            first_offset,
            inner_matrix,
            inner_bias,
            outer_matrix,
            outer_bias,
            second_scale,
            second_offset,
        ),
        ("ctx", "seq"),
    )
    return (
        layer_out.astype(jnp.bfloat16).reshape(seqs, block, width),
        tokens_grad.reshape(seqs, block, width),
    ) + tuple(finals)


def solution(mesh):
    return jax.shard_map(
        local,
        mesh=mesh,
        in_specs=(
            P(("seq", "fsdp"), "ctx", None),
            P(("seq", "fsdp"), "ctx", None),
            P("fsdp", None),
            P("fsdp", None),
            P("fsdp", None),
            P("fsdp", None),
            P("fsdp"),
            P("fsdp"),
            P("fsdp"),
            P("fsdp"),
            P("fsdp"),
            P("fsdp", None),
            P("fsdp"),
            P("fsdp", None),
            P("fsdp"),
            P("fsdp"),
            P("fsdp"),
        ),
        out_specs=(
            P(("seq", "fsdp"), "ctx", None),
            P(("seq", "fsdp"), "ctx", None),
            P("fsdp", None),
            P("fsdp", None),
            P("fsdp", None),
            P("fsdp", None),
            P("fsdp"),
            P("fsdp"),
            P("fsdp"),
            P("fsdp"),
            P("fsdp"),
            P("fsdp", None),
            P("fsdp"),
            P("fsdp", None),
            P("fsdp"),
            P("fsdp"),
            P("fsdp"),
        ),
        check_vma=False,
    )
```

profile of v0, /device:TPU:0, one launch (start us, length us, event | category | flops | bytes accessed | tf_op | source)
XLA Modules:
  0.0 1809.2 jit_solution(1213545254661435694)
XLA Ops:
  9.5 5.8 all-gather.2
  15.4 23.6 %all-gather.20.cloned.1.call-done = bf16[768,768]{1,0:T(8,128)(2,1)} async-done(((bf16[384,768]{1,0:T(8,128)(2,1)}), bf16[768,768]{1,0:T(8,128)(2,1)}) %all-gather.20.cloned.1.call-update) | async-done | bytes 1179664 | tf_op jit(solution)/shard_map/all_gather | solution.py:89
  41.3 25.6 %all-gather.24.cloned.1.call-done = bf16[768,768]{1,0:T(8,128)(2,1)} async-done(((bf16[384,768]{1,0:T(8,128)(2,1)}), bf16[768,768]{1,0:T(8,128)(2,1)}) %all-gather.24.cloned.1.call-update) | async-done | bytes 1179664 | tf_op jit(solution)/shard_map/all_gather | solution.py:88
  77.4 5.9 all-gather.7
  83.3 5.8 all-gather.4
  106.9 5.8 all-gather.9
  112.8 5.8 all-gather.10
  120.5 150.1 %all-gather.32.cloned.1.call-done = bf16[4096,768]{1,0:T(8,128)(2,1)} async-done(((bf16[128,768]{1,0:T(8,128)(2,1)}), bf16[4096,768]{1,0:T(8,128)(2,1)}) %all-gather.32.cloned.1.call-update) | async-done | bytes 6291472 | tf_op jit(solution)/shard_map/all_gather | solution.py:103
  270.5 8.7 copy.44
  279.2 166.5 %all-gather.34.cloned.1.call-done = bf16[4096,768]{1,0:T(8,128)(2,1)} async-done(((bf16[128,768]{1,0:T(8,128)(2,1)}), bf16[4096,768]{1,0:T(8,128)(2,1)}) %all-gather.34.cloned.1.call-update) | async-done | bytes 6291472 | tf_op jit(solution)/shard_map/all_gather | solution.py:102
  445.8 8.6 copy.46
  454.4 33.8 %while.26 = (s32[]{:T(128)}, bf16[6,1,128,128]{2,3,1,0:T(8,128)(2,1)S(1)}, f32[6,1,2,128]{3,2,1,0:T(2,128)S(1)}, s32[6]{0:T(128)S(1)}, bf16[1,4096,768]{1,2,0:T(...) while((s32[]{:T(128)}, ...), condition=%wide.region_3.4_spmd, body=%wide.region_0.3_spmd.sunk | while | flops 275775232 | bytes 19079360 | solution.py:120
  490.3 49.7 %all-gather.28.cloned.1.call-done = bf16[768,3072]{1,0:T(8,128)(2,1)} async-done(((bf16[384,3072]{1,0:T(8,128)(2,1)}), bf16[768,3072]{1,0:T(8,128)(2,1)}) %all-gather.28.cloned.1.call-update) | async-done | bytes 4718608 | tf_op jit(solution)/shard_map/all_gather | solution.py:126
  540.0 8.4 multiply_convert_fusion.1
  548.4 59.5 %all-gather.30.cloned.1.call-done = bf16[3072,768]{1,0:T(8,128)(2,1)} async-done(((bf16[1536,768]{1,0:T(8,128)(2,1)}), bf16[3072,768]{1,0:T(8,128)(2,1)}) %all-gather.30.cloned.1.call-update) | async-done | bytes 4718608 | tf_op jit(solution)/shard_map/all_gather | solution.py:128
  619.1 72.0 %while.27 = (s32[]{:T(128)}, bf16[6,1,128,128]{2,3,1,0:T(8,128)(2,1)S(1)}, bf16[6,1,4096,128]{2,3,1,0:T(8,128)(2,1)}, bf16[6,1,4096,128]{2,3,1,0:T(8,128)(2,1)},...) while((s32[]{:T(128)}, ...), condition=%wide.region_14.15_spmd, body=%wide.region_12.14_spmd.sunk | while | flops 680558336 | bytes 47093020 | solution.py:186
  691.1 27.8 %copy.54 = bf16[6,1,4096,128]{3,1,0,2:T(2,128)(2,1)} copy(bf16[6,1,4096,128]{2,3,1,0:T(8,128)(2,1)} %get-tuple-element.112) | data formatting | bytes 12582912
  718.9 110.1 %bitcast_reduce_fusion.1 = bf16[4096,6,128]{2,1,0:T(8,128)(2,1)} fusion(bf16[6,1,4096,128]{3,1,0,2:T(2,128)(2,1)} %copy.54), kind=kLoop, calls=%fused_computation.29 | loop fusion | bytes 12582912
  829.1 7.6 copy.172
  836.8 27.9 %copy.56 = bf16[6,1,4096,128]{3,1,0,2:T(2,128)(2,1)} copy(bf16[6,1,4096,128]{2,3,1,0:T(8,128)(2,1)} %get-tuple-element.113) | data formatting | bytes 12582912
  864.6 110.0 %bitcast_reduce_fusion = bf16[4096,6,128]{2,1,0:T(8,128)(2,1)} fusion(bf16[6,1,4096,128]{3,1,0,2:T(2,128)(2,1)} %copy.56), kind=kLoop, calls=%fused_computation.28 | loop fusion | bytes 12582912
  974.6 7.7 copy.171
  995.5 21.0 %reduce-scatter.25.cloned.1.call-done = bf16[128,768]{1,0:T(8,128)(2,1)} async-done(((bf16[4096,768]{1,0:T(8,128)(2,1)}), bf16[128,768]{1,0:T(8,128)(2,1)}) %reduce-scatter.25.cloned.1.call-update) | async-done | bytes 196624
  1020.3 176.3 %reduce-scatter.27.cloned.1.call-done = bf16[128,768]{1,0:T(8,128)(2,1)} async-done(((bf16[4096,768]{1,0:T(8,128)(2,1)}), bf16[128,768]{1,0:T(8,128)(2,1)}) %reduce-scatter.27.cloned.1.call-update) | async-done | bytes 196624
  1203.8 18.1 reduce-scatter.29.cloned.1.call-done
  1223.3 26.8 %reduce-scatter.19.cloned.1.call-done = bf16[384,768]{1,0:T(8,128)(2,1)} async-done(((bf16[768,768]{1,0:T(8,128)(2,1)}), bf16[384,768]{1,0:T(8,128)(2,1)}) %reduce-scatter.19.cloned.1.call-update) | async-done | bytes 589840 | tf_op jit(solution)/shard_map/reduce_scatter | solution.py:235
  1250.1 66.5 %reduce-scatter.21.cloned.1.call-done = bf16[384,3072]{1,0:T(8,128)(2,1)} async-done(((bf16[768,3072]{1,0:T(8,128)(2,1)}), bf16[384,3072]{1,0:T(8,128)(2,1)}) %reduce-scatter.21.cloned.1.call-update) | async-done | bytes 2359312 | tf_op jit(solution)/shard_map/reduce_scatter | solution.py:253
  1316.5 66.5 %reduce-scatter.23.cloned.1.call-done = bf16[1536,768]{1,0:T(8,128)(2,1)} async-done(((bf16[3072,768]{1,0:T(8,128)(2,1)}), bf16[1536,768]{1,0:T(8,128)(2,1)}) %reduce-scatter.23.cloned.1.call-update) | async-done | bytes 2359312 | tf_op jit(solution)/shard_map/reduce_scatter | solution.py:259
  1383.2 8.6 all-reduce.10
  1395.3 15.8 reduce-scatter.31.cloned.1.call-done
  1412.4 26.8 %reduce-scatter.33.cloned.1.call-done = bf16[384,768]{1,0:T(8,128)(2,1)} async-done(((bf16[768,768]{1,0:T(8,128)(2,1)}), bf16[384,768]{1,0:T(8,128)(2,1)}) %reduce-scatter.33.cloned.1.call-update) | async-done | bytes 589840
  1440.6 356.2 %all-reduce.12 = (f32[384,768]{0,1:T(8,128)}, f32[384,768]{0,1:T(8,128)}, f32[384,768]{0,1:T(8,128)S(1)}, f32[384,768]{1,0:T(8,128)}, f32[384]{0:T(512)}, /*inde...) all-reduce(bf16[384,768]{0,1:T(8,128)(2,1)S(1)} %copy.59, ...), channel_id=1, replica_groups=mesh['ctx'=32,'seq'=2,'fsdp'=2] {'ctx','seq'}, use_global_device_ids=true, to_apply=%region_18.19 | all-reduce | flops 3543552 | bytes 21270528 | tf_op jit(solution)/shard_map/psum | solution.py:272
  (351 shorter events, 180.4 us)
Async XLA Ops:
  7.2 31.8 %copy-start = (bf16[1,128,768]{2,1,0:T(8,128)(2,1)S(1)}, bf16[1,128,768]{2,1,0:T(8,128)(2,1)}, u32[]{:S(2)}) copy-start(bf16[1,128,768]{2,1,0:T(8,128)(2,1)} %param.21) | copy-start | bytes 589828
  7.2 31.8 %all-gather.20.cloned.1.call-start = ((), (), s32[]{:S(2)}) async-start(), calls=%async_computation.8 | async-start | bytes 1769472 | tf_op jit(solution)/shard_map/all_gather | solution.py:89
  7.9 59.0 %all-gather.24.cloned.1.call-start = ((), (), s32[]{:S(2)}) async-start(), calls=%async_computation.10 | async-start | bytes 1769472 | tf_op jit(solution)/shard_map/all_gather | solution.py:88
  8.7 110.0 %all-gather.22.cloned.1.call-start = ((), (), s32[]{:S(2)}) async-start(), calls=%async_computation.9 | async-start | bytes 1769472 | tf_op jit(solution)/shard_map/all_gather | solution.py:87
  9.4 261.1 %all-gather.32.cloned.1.call-start = ((), (), s32[]{:S(2)}) async-start(), calls=%async_computation.17 | async-start | bytes 6488064 | tf_op jit(solution)/shard_map/all_gather | solution.py:103
  41.3 404.5 %all-gather.34.cloned.1.call-start = ((), (), s32[]{:S(2)}) async-start(), calls=%async_computation.18 | async-start | bytes 6488064 | tf_op jit(solution)/shard_map/all_gather | solution.py:102
  69.2 419.0 %all-gather.26.cloned.1.call-start = ((), (), s32[]{:S(2)}) async-start(), calls=%async_computation.11 | async-start | bytes 1769472 | tf_op jit(solution)/shard_map/all_gather | solution.py:90
  69.8 470.2 %all-gather.28.cloned.1.call-start = ((), (), s32[]{:S(2)}) async-start(), calls=%async_computation.12 | async-start | bytes 7077888 | tf_op jit(solution)/shard_map/all_gather | solution.py:126
  70.6 6.8 copy-start.16
  70.6 12.7 copy-start.19
  70.6 18.6 %copy-start.20 = (bf16[384]{0:T(512)(128)(2,1)S(1)}, bf16[384]{0:T(512)(128)(2,1)}, u32[]{:S(2)}) copy-start(bf16[384]{0:T(512)(128)(2,1)} %param.27) | copy-start | bytes 2308
  70.6 24.5 %copy-start.21 = (bf16[384]{0:T(512)(128)(2,1)S(1)}, bf16[384]{0:T(512)(128)(2,1)}, u32[]{:S(2)}) copy-start(bf16[384]{0:T(512)(128)(2,1)} %param.31) | copy-start | bytes 2308
  70.6 30.3 %copy-start.22 = (bf16[384]{0:T(512)(128)(2,1)S(1)}, bf16[384]{0:T(512)(128)(2,1)}, u32[]{:S(2)}) copy-start(bf16[384]{0:T(512)(128)(2,1)} %param.30) | copy-start | bytes 2308
  70.6 36.2 %copy-start.23 = (bf16[384]{0:T(512)(128)(2,1)S(1)}, bf16[384]{0:T(512)(128)(2,1)}, u32[]{:S(2)}) copy-start(bf16[384]{0:T(512)(128)(2,1)} %param.36) | copy-start | bytes 2308
  70.6 42.1 %copy-start.24 = (bf16[384]{0:T(512)(128)(2,1)S(1)}, bf16[384]{0:T(512)(128)(2,1)}, u32[]{:S(2)}) copy-start(bf16[384]{0:T(512)(128)(2,1)} %param.37) | copy-start | bytes 2308
  70.7 537.2 %all-gather.30.cloned.1.call-start = ((), (), s32[]{:S(2)}) async-start(), calls=%async_computation.13 | async-start | bytes 7077888 | tf_op jit(solution)/shard_map/all_gather | solution.py:128
  71.4 945.1 %reduce-scatter.25.cloned.1.call-start = ((), (), s32[]{:S(2)}) async-start(), calls=%async_computation.19 | async-start | bytes 6488064
  488.2 60.2 %copy-start.7 = (bf16[6,1,128,128]{2,3,1,0:T(8,128)(2,1)}, bf16[6,1,128,128]{2,3,1,0:T(8,128)(2,1)S(1)}, u32[]{:S(2)}) copy-start(bf16[6,1,128,128]{2,3,1,0:T(8,128)(2,1)S(1)} %get-tuple-element.109) | copy-start | bytes 589828
  607.8 4.7 slice-start.2
  607.8 4.7 slice-start.3
  607.8 4.7 copy-start.27
  836.7 359.9 %reduce-scatter.27.cloned.1.call-start = ((), (), s32[]{:S(2)}) async-start(), calls=%async_computation.20 | async-start | bytes 6488064
  982.3 239.6 %reduce-scatter.29.cloned.1.call-start = ((), (), s32[]{:S(2)}) async-start(), calls=%async_computation.21 | async-start | bytes 1769472
  986.3 263.8 %reduce-scatter.19.cloned.1.call-start = ((), (), s32[]{:S(2)}) async-start(), calls=%async_computation.14 | async-start | bytes 1769472 | tf_op jit(solution)/shard_map/reduce_scatter | solution.py:235
  988.0 328.5 %reduce-scatter.21.cloned.1.call-start = ((), (), s32[]{:S(2)}) async-start(), calls=%async_computation.15 | async-start | bytes 7077888 | tf_op jit(solution)/shard_map/reduce_scatter | solution.py:253
  991.8 391.2 %reduce-scatter.23.cloned.1.call-start = ((), (), s32[]{:S(2)}) async-start(), calls=%async_computation.16 | async-start | bytes 7077888 | tf_op jit(solution)/shard_map/reduce_scatter | solution.py:259
  995.5 415.5 %reduce-scatter.31.cloned.1.call-start = ((), (), s32[]{:S(2)}) async-start(), calls=%async_computation.22 | async-start | bytes 1769472
  1020.3 418.9 %reduce-scatter.33.cloned.1.call-start = ((), (), s32[]{:S(2)}) async-start(), calls=%async_computation.23 | async-start | bytes 1769472
  1198.9 3.6 copy-start.3
  1202.5 189.9 %copy-start.2 = (bf16[768,768]{1,0:T(8,128)(2,1)S(1)}, bf16[768,768]{1,0:T(8,128)(2,1)}, u32[]{:S(2)}) copy-start(bf16[768,768]{1,0:T(8,128)(2,1)} %all-gather.24.cloned.1.call-done) | copy-start | bytes 3538948
  1203.8 188.7 %copy-start.10 = (bf16[6,1,128,128]{2,3,1,0:T(8,128)(2,1)S(1)}, bf16[6,1,128,128]{2,3,1,0:T(8,128)(2,1)}, u32[]{:S(2)}) copy-start(bf16[6,1,128,128]{2,3,1,0:T(8,128)(2,1)} %copy-done.9) | copy-start | bytes 589828
  1203.8 190.2 %copy-start.1 = (bf16[768,768]{1,0:T(8,128)(2,1)S(1)}, bf16[768,768]{1,0:T(8,128)(2,1)}, u32[]{:S(2)}) copy-start(bf16[768,768]{1,0:T(8,128)(2,1)} %all-gather.20.cloned.1.call-done) | copy-start | bytes 3538948
  (26 other events, 44.7 us)
Sparse Core Ops, SparseCore 0:
  9.7 29.2 all-gather.19
  40.6 26.2 all-gather.23
  68.6 26.3 all-gather.21
  97.1 173.4 all-gather.31
  272.6 173.1 all-gather.33
  447.3 24.7 all-gather.25
  473.7 66.2 all-gather.27
  541.6 66.1 all-gather.29
  836.8 179.6 reduce-scatter.24
  1018.8 177.7 reduce-scatter.26
  1199.5 22.3 reduce-scatter.28
  1224.8 25.2 reduce-scatter.18
  1253.0 63.4 reduce-scatter.20
  1319.5 63.4 reduce-scatter.22
  1385.8 25.2 reduce-scatter.30
  1413.9 25.2 reduce-scatter.32
where the time goes:
time: 1820 us; the launch traced here: 1810 us
  waiting for transfers between devices  897 us (49%)
  blocking collectives  417 us (23%)
  local copies, waits for them, and re-layouts  382 us (21%)
  matrix products  74.2 us (4%)
    psum x1, blocking collectives, local(): lax.psum((query_matrix, keys_matrix, value_matrix, output_matrix, query_b...  356 us
    unnamed x89, local copies, waits for them, and re-layouts  312 us
    unnamed x21, waiting for transfers between devices  262 us
    all_gather x1, waiting for transfers between devices, local(): lax.all_gather(keys, 'ctx', axis=1, tiled=True)  167 us
    all_gather x1, waiting for transfers between devices, local(): lax.all_gather(values, 'ctx', axis=1, tiled=True)  150 us
    reduce_scatter x1, waiting for transfers between devices, local(): lax.psum_scatter(outer_matrix.astype(jnp.bfloat16), 'fsdp', scatter_dimen...  66.5 us
    reduce_scatter x1, waiting for transfers between devices, local(): lax.psum_scatter(inner_matrix.astype(jnp.bfloat16), 'fsdp', scatter_dimen...  66.5 us
    all_gather x1, waiting for transfers between devices, local(): lax.all_gather(w_outer, 'fsdp', axis=0, tiled=True)  59.5 us
  transfers between devices with their start and end apart: 16, of which 14 were waited for; matrix products, arithmetic and copies ran while one was open for 13% of the time, Pallas kernels for 0%

commit v1 on v0

--- a/solution.py
+++ b/solution.py
@@ -270,24 +270,27 @@
         ).astype(jnp.float32),
     )
     finals = lax.psum(
-        (
-            query_matrix,
-            keys_matrix,
-            value_matrix,
-            output_matrix,
-            query_bias,
-            value_bias,
-            output_bias,
-            first_scale,
-            first_offset,
-            inner_matrix,
-            inner_bias,
-            outer_matrix,
-            outer_bias,
-            second_scale,
-            second_offset,
+        lax.psum(
+            (
+                query_matrix,
+                keys_matrix,
+                value_matrix,
+                output_matrix,
+                query_bias,
+                value_bias,
+                output_bias,
+                first_scale,
+                first_offset,
+                inner_matrix,
+                inner_bias,
+                outer_matrix,
+                outer_bias,
+                second_scale,
+                second_offset,
+            ),
+            "ctx",
         ),
-        ("ctx", "seq"),
+        "seq",
     )
     return (
         layer_out.astype(jnp.bfloat16).reshape(seqs, block, width),

time: 1820 us -> 2140 us (1.18)
  blocking collectives: 417 us -> 672 us
  waiting for transfers between devices: 897 us -> 952 us
    psum x1, blocking collectives: 356 us -> 607 us  [local(): lax.psum((query_matrix, keys_matrix, value_matrix, output_matrix, query_b...]
    psum x0 -> x1, waiting for transfers between devices: none -> 48.6 us  [local(): lax.psum(lax.psum((query_matrix, keys_matrix, value_matrix, output_matrix...]
    unnamed x89 -> x96, local copies, waits for them, and re-layouts: 312 us -> 323 us
    unnamed x21 -> x22, waiting for transfers between devices: 262 us -> 268 us
  transfers between devices with their start and end apart: 16 -> 17, of which waited for: 14 -> 15; matrix products, arithmetic and copies ran while one was open for 13% -> 11% of each run, Pallas kernels for 0% -> 0%
where the time goes in v1:
time: 2140 us; the launch traced here: 2130 us
  waiting for transfers between devices  952 us (44%)
  blocking collectives  672 us (31%)
  local copies, waits for them, and re-layouts  393 us (18%)
  matrix products  72.4 us (3%)
    psum x1, blocking collectives, local(): lax.psum((query_matrix, keys_matrix, value_matrix, output_matrix, query_b...  607 us
    unnamed x96, local copies, waits for them, and re-layouts  323 us
    unnamed x22, waiting for transfers between devices  268 us
    all_gather x1, waiting for transfers between devices, local(): lax.all_gather(keys, 'ctx', axis=1, tiled=True)  167 us
    all_gather x1, waiting for transfers between devices, local(): lax.all_gather(values, 'ctx', axis=1, tiled=True)  150 us
    reduce_scatter x1, waiting for transfers between devices, local(): lax.psum_scatter(outer_matrix.astype(jnp.bfloat16), 'fsdp', scatter_dimen...  66.5 us
    reduce_scatter x1, waiting for transfers between devices, local(): lax.psum_scatter(inner_matrix.astype(jnp.bfloat16), 'fsdp', scatter_dimen...  66.5 us
    all_gather x1, waiting for transfers between devices, local(): lax.all_gather(w_outer, 'fsdp', axis=0, tiled=True)  59.5 us
  transfers between devices with their start and end apart: 17, of which 15 were waited for; matrix products, arithmetic and copies ran while one was open for 11% of the time, Pallas kernels for 0%

profile of v1, /device:TPU:0, one launch (start us, length us, event | category | flops | bytes accessed | tf_op | source)
XLA Modules:
  0.0 2128.9 jit_solution(12225661135092517761)
XLA Ops:
  15.4 23.6 %all-gather.20.cloned.1.call-done = bf16[768,768]{1,0:T(8,128)(2,1)} async-done(((bf16[384,768]{1,0:T(8,128)(2,1)}), bf16[768,768]{1,0:T(8,128)(2,1)}) %all-gather.20.cloned.1.call-update) | async-done | bytes 1179664 | tf_op jit(solution)/shard_map/all_gather | solution.py:89
  41.3 25.6 %all-gather.24.cloned.1.call-done = bf16[768,768]{1,0:T(8,128)(2,1)} async-done(((bf16[384,768]{1,0:T(8,128)(2,1)}), bf16[768,768]{1,0:T(8,128)(2,1)}) %all-gather.24.cloned.1.call-update) | async-done | bytes 1179664 | tf_op jit(solution)/shard_map/all_gather | solution.py:88
  77.4 5.9 all-gather.7
  83.3 5.8 all-gather.4
  106.9 5.8 all-gather.9
  112.8 5.8 all-gather.10
  120.5 150.1 %all-gather.32.cloned.1.call-done = bf16[4096,768]{1,0:T(8,128)(2,1)} async-done(((bf16[128,768]{1,0:T(8,128)(2,1)}), bf16[4096,768]{1,0:T(8,128)(2,1)}) %all-gather.32.cloned.1.call-update) | async-done | bytes 6291472 | tf_op jit(solution)/shard_map/all_gather | solution.py:103
  270.5 8.7 copy.44
  279.2 166.5 %all-gather.34.cloned.1.call-done = bf16[4096,768]{1,0:T(8,128)(2,1)} async-done(((bf16[128,768]{1,0:T(8,128)(2,1)}), bf16[4096,768]{1,0:T(8,128)(2,1)}) %all-gather.34.cloned.1.call-update) | async-done | bytes 6291472 | tf_op jit(solution)/shard_map/all_gather | solution.py:102
  445.8 8.6 copy.46
  454.4 33.8 %while.26 = (s32[]{:T(128)}, bf16[6,1,128,128]{2,3,1,0:T(8,128)(2,1)S(1)}, f32[6,1,2,128]{3,2,1,0:T(2,128)S(1)}, s32[6]{0:T(128)S(1)}, bf16[1,4096,768]{1,2,0:T(...) while((s32[]{:T(128)}, ...), condition=%wide.region_3.4_spmd, body=%wide.region_0.3_spmd.sunk | while | flops 275775232 | bytes 19079360 | solution.py:120
  490.3 49.7 %all-gather.28.cloned.1.call-done = bf16[768,3072]{1,0:T(8,128)(2,1)} async-done(((bf16[384,3072]{1,0:T(8,128)(2,1)}), bf16[768,3072]{1,0:T(8,128)(2,1)}) %all-gather.28.cloned.1.call-update) | async-done | bytes 4718608 | tf_op jit(solution)/shard_map/all_gather | solution.py:126
  540.0 8.4 multiply_convert_fusion.1
  548.4 59.5 %all-gather.30.cloned.1.call-done = bf16[3072,768]{1,0:T(8,128)(2,1)} async-done(((bf16[1536,768]{1,0:T(8,128)(2,1)}), bf16[3072,768]{1,0:T(8,128)(2,1)}) %all-gather.30.cloned.1.call-update) | async-done | bytes 4718608 | tf_op jit(solution)/shard_map/all_gather | solution.py:128
  619.1 72.0 %while.27 = (s32[]{:T(128)}, bf16[6,1,128,128]{2,3,1,0:T(8,128)(2,1)S(1)}, bf16[6,1,4096,128]{2,3,1,0:T(8,128)(2,1)}, bf16[6,1,4096,128]{2,3,1,0:T(8,128)(2,1)},...) while((s32[]{:T(128)}, ...), condition=%wide.region_14.15_spmd, body=%wide.region_12.14_spmd.sunk | while | flops 680558336 | bytes 47093020 | solution.py:186
  691.1 27.8 %copy.54 = bf16[6,1,4096,128]{3,1,0,2:T(2,128)(2,1)} copy(bf16[6,1,4096,128]{2,3,1,0:T(8,128)(2,1)} %get-tuple-element.112) | data formatting | bytes 12582912
  718.9 110.1 %bitcast_reduce_fusion.1 = bf16[4096,6,128]{2,1,0:T(8,128)(2,1)} fusion(bf16[6,1,4096,128]{3,1,0,2:T(2,128)(2,1)} %copy.54), kind=kLoop, calls=%fused_computation.29 | loop fusion | bytes 12582912
  829.1 7.6 copy.172
  836.8 27.9 %copy.56 = bf16[6,1,4096,128]{3,1,0,2:T(2,128)(2,1)} copy(bf16[6,1,4096,128]{2,3,1,0:T(8,128)(2,1)} %get-tuple-element.113) | data formatting | bytes 12582912
  864.6 110.0 %bitcast_reduce_fusion = bf16[4096,6,128]{2,1,0:T(8,128)(2,1)} fusion(bf16[6,1,4096,128]{3,1,0,2:T(2,128)(2,1)} %copy.56), kind=kLoop, calls=%fused_computation.28 | loop fusion | bytes 12582912
  974.6 7.7 copy.171
  995.6 21.5 %reduce-scatter.25.cloned.1.call-done = bf16[128,768]{1,0:T(8,128)(2,1)} async-done(((bf16[4096,768]{1,0:T(8,128)(2,1)}), bf16[128,768]{1,0:T(8,128)(2,1)}) %reduce-scatter.25.cloned.1.call-update) | async-done | bytes 196624
  1020.8 177.5 %reduce-scatter.27.cloned.1.call-done = bf16[128,768]{1,0:T(8,128)(2,1)} async-done(((bf16[4096,768]{1,0:T(8,128)(2,1)}), bf16[128,768]{1,0:T(8,128)(2,1)}) %reduce-scatter.27.cloned.1.call-update) | async-done | bytes 196624
  1204.3 19.7 reduce-scatter.29.cloned.1.call-done
  1225.4 26.8 %reduce-scatter.19.cloned.1.call-done = bf16[384,768]{1,0:T(8,128)(2,1)} async-done(((bf16[768,768]{1,0:T(8,128)(2,1)}), bf16[384,768]{1,0:T(8,128)(2,1)}) %reduce-scatter.19.cloned.1.call-update) | async-done | bytes 589840 | tf_op jit(solution)/shard_map/reduce_scatter | solution.py:235
  1252.2 66.5 %reduce-scatter.21.cloned.1.call-done = bf16[384,3072]{1,0:T(8,128)(2,1)} async-done(((bf16[768,3072]{1,0:T(8,128)(2,1)}), bf16[384,3072]{1,0:T(8,128)(2,1)}) %reduce-scatter.21.cloned.1.call-update) | async-done | bytes 2359312 | tf_op jit(solution)/shard_map/reduce_scatter | solution.py:253
  1318.6 66.5 %reduce-scatter.23.cloned.1.call-done = bf16[1536,768]{1,0:T(8,128)(2,1)} async-done(((bf16[3072,768]{1,0:T(8,128)(2,1)}), bf16[1536,768]{1,0:T(8,128)(2,1)}) %reduce-scatter.23.cloned.1.call-update) | async-done | bytes 2359312 | tf_op jit(solution)/shard_map/reduce_scatter | solution.py:259
  1385.3 8.6 all-reduce.12
  1394.5 18.6 reduce-scatter.31.cloned.1.call-done
  1414.5 26.8 %reduce-scatter.33.cloned.1.call-done = bf16[384,768]{1,0:T(8,128)(2,1)} async-done(((bf16[768,768]{1,0:T(8,128)(2,1)}), bf16[384,768]{1,0:T(8,128)(2,1)}) %reduce-scatter.33.cloned.1.call-update) | async-done | bytes 589840
  1442.7 607.2 %all-reduce.17 = (f32[384,768]{0,1:T(8,128)}, f32[384,768]{0,1:T(8,128)}, f32[384,768]{0,1:T(8,128)}, f32[384,768]{1,0:T(8,128)}, f32[384]{0:T(512)S(1)}, /*inde...) all-reduce(bf16[384,768]{0,1:T(8,128)(2,1)S(1)} %copy.59, ...), channel_id=1, replica_groups=mesh['ctx'=32,'seq'=2,'fsdp'=2] {'ctx'}, use_global_device_ids=true, to_apply=%region_18.19 | all-reduce | flops 3543552 | bytes 21270528 | tf_op jit(solution)/shard_map/psum | solution.py:273
  2059.0 48.6 %all-reduce.16.cloned.1.call-done = (f32[384,768]{0,1:T(8,128)}, f32[384,768]{0,1:T(8,128)}, f32[384,768]{0,1:T(8,128)}, f32[384,768]{1,0:T(8,128)}, f32[384,3072]{1,0:T(8,128)}, /*index=5*/f32[1536,768]{1,0:T(8,128)}) async-done(((f32[384,768]{0,1:T(8,128)}, f32[384,768]{0,1:T(8,128)}, f32[384,768]{0,1:T(8,128)}, f32[384,768]{1,0:T(8,128)}, f32[384,3072]{1,0:T(8,128)}, /*index=5*/f32[1536,768]{1,0:T(8,128)}), ...) | async-done | bytes 14155792 | tf_op jit(solution)/shard_map/psum | solution.py:272
  (363 shorter events, 200.2 us)
Async XLA Ops:
  7.2 31.8 %copy-start = (bf16[1,128,768]{2,1,0:T(8,128)(2,1)S(1)}, bf16[1,128,768]{2,1,0:T(8,128)(2,1)}, u32[]{:S(2)}) copy-start(bf16[1,128,768]{2,1,0:T(8,128)(2,1)} %param.21) | copy-start | bytes 589828
  7.2 31.8 %all-gather.20.cloned.1.call-start = ((), (), s32[]{:S(2)}) async-start(), calls=%async_computation.8 | async-start | bytes 1769472 | tf_op jit(solution)/shard_map/all_gather | solution.py:89
  7.9 59.0 %all-gather.24.cloned.1.call-start = ((), (), s32[]{:S(2)}) async-start(), calls=%async_computation.10 | async-start | bytes 1769472 | tf_op jit(solution)/shard_map/all_gather | solution.py:88
  8.7 110.0 %all-gather.22.cloned.1.call-start = ((), (), s32[]{:S(2)}) async-start(), calls=%async_computation.9 | async-start | bytes 1769472 | tf_op jit(solution)/shard_map/all_gather | solution.py:87
  9.4 261.1 %all-gather.32.cloned.1.call-start = ((), (), s32[]{:S(2)}) async-start(), calls=%async_computation.17 | async-start | bytes 6488064 | tf_op jit(solution)/shard_map/all_gather | solution.py:103
  41.3 404.5 %all-gather.34.cloned.1.call-start = ((), (), s32[]{:S(2)}) async-start(), calls=%async_computation.18 | async-start | bytes 6488064 | tf_op jit(solution)/shard_map/all_gather | solution.py:102
  69.2 419.0 %all-gather.26.cloned.1.call-start = ((), (), s32[]{:S(2)}) async-start(), calls=%async_computation.11 | async-start | bytes 1769472 | tf_op jit(solution)/shard_map/all_gather | solution.py:90
  69.8 470.2 %all-gather.28.cloned.1.call-start = ((), (), s32[]{:S(2)}) async-start(), calls=%async_computation.12 | async-start | bytes 7077888 | tf_op jit(solution)/shard_map/all_gather | solution.py:126
  70.6 6.8 copy-start.16
  70.6 12.7 copy-start.19
  70.6 18.6 copy-start.20
  70.6 24.5 %copy-start.21 = (bf16[384]{0:T(512)(128)(2,1)S(1)}, bf16[384]{0:T(512)(128)(2,1)}, u32[]{:S(2)}) copy-start(bf16[384]{0:T(512)(128)(2,1)} %param.31) | copy-start | bytes 2308
  70.6 30.3 %copy-start.22 = (bf16[384]{0:T(512)(128)(2,1)S(1)}, bf16[384]{0:T(512)(128)(2,1)}, u32[]{:S(2)}) copy-start(bf16[384]{0:T(512)(128)(2,1)} %param.30) | copy-start | bytes 2308
  70.6 36.2 %copy-start.23 = (bf16[384]{0:T(512)(128)(2,1)S(1)}, bf16[384]{0:T(512)(128)(2,1)}, u32[]{:S(2)}) copy-start(bf16[384]{0:T(512)(128)(2,1)} %param.36) | copy-start | bytes 2308
  70.6 42.1 %copy-start.24 = (bf16[384]{0:T(512)(128)(2,1)S(1)}, bf16[384]{0:T(512)(128)(2,1)}, u32[]{:S(2)}) copy-start(bf16[384]{0:T(512)(128)(2,1)} %param.37) | copy-start | bytes 2308
  70.7 537.2 %all-gather.30.cloned.1.call-start = ((), (), s32[]{:S(2)}) async-start(), calls=%async_computation.13 | async-start | bytes 7077888 | tf_op jit(solution)/shard_map/all_gather | solution.py:128
  71.4 945.6 %reduce-scatter.25.cloned.1.call-start = ((), (), s32[]{:S(2)}) async-start(), calls=%async_computation.19 | async-start | bytes 6488064
  488.2 60.2 %copy-start.7 = (bf16[6,1,128,128]{2,3,1,0:T(8,128)(2,1)}, bf16[6,1,128,128]{2,3,1,0:T(8,128)(2,1)S(1)}, u32[]{:S(2)}) copy-start(bf16[6,1,128,128]{2,3,1,0:T(8,128)(2,1)S(1)} %get-tuple-element.109) | copy-start | bytes 589828
  607.8 4.7 slice-start.2
  607.8 3.6 copy-start.9
  607.8 4.7 slice-start.3
  607.8 4.7 copy-start.27
  836.7 361.6 %reduce-scatter.27.cloned.1.call-start = ((), (), s32[]{:S(2)}) async-start(), calls=%async_computation.20 | async-start | bytes 6488064
  982.3 241.7 %reduce-scatter.29.cloned.1.call-start = ((), (), s32[]{:S(2)}) async-start(), calls=%async_computation.21 | async-start | bytes 1769472
  986.3 265.9 %reduce-scatter.19.cloned.1.call-start = ((), (), s32[]{:S(2)}) async-start(), calls=%async_computation.14 | async-start | bytes 1769472 | tf_op jit(solution)/shard_map/reduce_scatter | solution.py:235
  988.0 330.6 %reduce-scatter.21.cloned.1.call-start = ((), (), s32[]{:S(2)}) async-start(), calls=%async_computation.15 | async-start | bytes 7077888 | tf_op jit(solution)/shard_map/reduce_scatter | solution.py:253
  991.8 393.3 %reduce-scatter.23.cloned.1.call-start = ((), (), s32[]{:S(2)}) async-start(), calls=%async_computation.16 | async-start | bytes 7077888 | tf_op jit(solution)/shard_map/reduce_scatter | solution.py:259
  995.5 417.6 %reduce-scatter.31.cloned.1.call-start = ((), (), s32[]{:S(2)}) async-start(), calls=%async_computation.22 | async-start | bytes 1769472
  1020.8 420.5 %reduce-scatter.33.cloned.1.call-start = ((), (), s32[]{:S(2)}) async-start(), calls=%async_computation.23 | async-start | bytes 1769472
  1202.1 905.4 %all-reduce.16.cloned.1.call-start = ((), (), s32[]{:S(2)}) async-start(), calls=%async_computation.24 | async-start | bytes 28311552 | tf_op jit(solution)/shard_map/psum | solution.py:272
  2113.1 6.7 slice-start.4
  2114.1 5.7 slice-start.5
  (29 other events, 45.8 us)
Sparse Core Ops, SparseCore 0:
  9.7 29.2 all-gather.19
  40.6 26.2 all-gather.23
  68.6 26.3 all-gather.21
  97.1 173.4 all-gather.31
  272.6 173.1 all-gather.33
  447.3 24.7 all-gather.25
  473.7 66.2 all-gather.27
  541.6 66.1 all-gather.29
  836.8 180.1 reduce-scatter.24
  1019.3 179.0 reduce-scatter.26
  1201.3 22.6 reduce-scatter.28
  1226.9 25.2 reduce-scatter.18
  1255.2 63.4 reduce-scatter.20
  1321.6 63.4 reduce-scatter.22
  1387.9 25.2 reduce-scatter.30
  1416.0 25.2 reduce-scatter.32
  2050.0 57.4 all-reduce.15
